TPU v7x, 128 devices: a whole 4x4x4 slice. The times are simulated.
128 devices in a mesh: exp: 4 (over x), tp: 32 (over z, y, core).
Axes of the slice: x: 4, y: 4, z: 4, core: 2. Of those that a mesh axis runs over, the one named last changes fastest.
Arguments:
- inputs: bfloat16 [1024, 4096], P(('exp', 'tp')), may hold values from -6 to 6
- conv_weight: float32 [4, 4096], replicated, may hold values from -3 to 3
- expert_ids: int32 [1024, 2], P(('exp', 'tp')), may hold values from 0 to 7, all different within a row; in each aligned block of 8 rows (0 to 7, 8 to 15, ...) at most 3 rows name the same one
- gate_values: float32 [1024, 2], P(('exp', 'tp')), may hold values from 0.25 to 1
- cotangent: bfloat16 [1024, 4096], P(('exp', 'tp')), may hold values from -6 to 6
- gate_weight: bfloat16 [8, 4096, 14336], P('exp', None, 'tp'), may hold values from -0.09375 to 0.09375
- up_weight: bfloat16 [8, 4096, 14336], P('exp', None, 'tp'), may hold values from -0.09375 to 0.09375
- down_weight: bfloat16 [8, 14336, 4096], P('exp', 'tp'), may hold values from -0.046875 to 0.046875
Outputs:
- result: bfloat16 [1024, 4096], P(('exp', 'tp'))
- grad_inputs: bfloat16 [1024, 4096], P(('exp', 'tp'))
Inputs may be any that keep to these rules, and one draw needn't show every extreme that they name: `expert_ids`: the experts of one token differ. Among the 8 tokens of one device no expert is named more than 3 times, a bound that some block reaches; every expert is named somewhere.
All inputs are finite; a program needn't handle non-finite values.
Results may differ from a plain program's by a relative error of at most 0.014.
Values may be sent and summed in bfloat16 or wider, within the bound.
A program may use at most 128 MiB of HBM per device.

v0:
```python
import jax
import jax.numpy as jnp
from jax import lax
from jax.sharding import PartitionSpec as P


def shifted(array, axis, by):
    size = lax.axis_size(axis)
    pairs = [(i, i + by) for i in range(size) if 0 <= i + by < size]
    return lax.ppermute(array, axis, pairs)


def expert_rows(rows_in, rows_grad, gate_weight, up_weight, down_weight):
    gate_pre = jnp.einsum(
        "mjsd,jdf->mjsf", rows_in, gate_weight, preferred_element_type=jnp.float32
    )
    up_pre = jnp.einsum("mjsd,jdf->mjsf", rows_in, up_weight, preferred_element_type=jnp.float32)
    sigmoid_gate = jax.nn.sigmoid(gate_pre)
    activated = gate_pre * sigmoid_gate
    hidden = (activated * up_pre).astype(jnp.bfloat16)
    forward_part = jnp.einsum(
        "mjsf,jfd->mjsd", hidden, down_weight, preferred_element_type=jnp.float32
    )
    back_hidden = jnp.einsum(
        "mjsd,jfd->mjsf", rows_grad, down_weight, preferred_element_type=jnp.float32
    )
    grad_gate = (
        back_hidden * up_pre * sigmoid_gate * (1.0 + gate_pre * (1.0 - sigmoid_gate))
    ).astype(jnp.bfloat16)
    grad_up = (back_hidden * activated).astype(jnp.bfloat16)
    backward_part = jnp.einsum(
        "mjsf,jdf->mjsd", grad_gate, gate_weight, preferred_element_type=jnp.float32
    ) + jnp.einsum("mjsf,jdf->mjsd", grad_up, up_weight, preferred_element_type=jnp.float32)
    return (forward_part, backward_part)


def per_device(
    inputs, conv_weight, expert_ids, gate_values, cotangent, gate_weight, up_weight, down_weight
):
    tok_rows = inputs.shape[0]
    model_width = inputs.shape[1]
    kernel = conv_weight.shape[0]
    top_count = expert_ids.shape[1]
    groups = lax.axis_size("exp")
    per_group = gate_weight.shape[0]
    experts = groups * per_group
    slot_count = tok_rows * top_count * 3 // (2 * experts)
    source = inputs.astype(jnp.float32)
    rim_rows = shifted(inputs[tok_rows - (kernel - 1) :], ("exp", "tp"), 1)
    extended = jnp.concatenate([rim_rows.astype(jnp.float32), source], 0)
    conv_sum = source
    for shift_step in range(kernel):
        conv_sum = (
            conv_sum
            + conv_weight[shift_step]
            * extended[kernel - 1 - shift_step : kernel - 1 - shift_step + tok_rows]
        )
    mixed = conv_sum.astype(jnp.bfloat16)
    flat_ids = expert_ids.reshape(-1)
    onehot_ids = (flat_ids[:, None] == jnp.arange(experts, dtype=jnp.int32)[None, :]).astype(
        jnp.int32
    )
    earlier = jnp.cumsum(onehot_ids, 0) - onehot_ids
    slot_index = jnp.sum(earlier * onehot_ids, 1)
    target = flat_ids * slot_count + slot_index
    places = (
        jnp.arange(experts * slot_count, dtype=jnp.int32)[:, None] == target[None, :]
    ).reshape(experts * slot_count, tok_rows, top_count)
    dispatch_map = jnp.any(places, 2).astype(jnp.bfloat16)
    packed_in = (
        jnp.dot(dispatch_map, mixed, preferred_element_type=jnp.float32)
        .astype(jnp.bfloat16)
        .reshape(groups, per_group, slot_count, model_width)
    )
    packed_grad = (
        jnp.dot(dispatch_map, cotangent, preferred_element_type=jnp.float32)
        .astype(jnp.bfloat16)
        .reshape(groups, per_group, slot_count, model_width)
    )
    recv_in, recv_grad = (
        lax.all_to_all(packed_in, "exp", split_axis=0, concat_axis=0, tiled=True),
        lax.all_to_all(packed_grad, "exp", split_axis=0, concat_axis=0, tiled=True),
    )
    stacked = jnp.stack([recv_in, recv_grad], 0)[None]
    piece = lax.all_gather(stacked, "tp", axis=0, tiled=True)
    piece_rows = piece.shape[0]
    rows_in = piece[:, 0].reshape(piece_rows * groups, per_group, slot_count, model_width)
    rows_grad = piece[:, 1].reshape(piece_rows * groups, per_group, slot_count, model_width)
    forward_part, backward_part = expert_rows(
        rows_in, rows_grad, gate_weight, up_weight, down_weight
    )
    shape_back = (piece_rows, groups, per_group, slot_count, model_width)
    partials = jnp.stack(
        [
            forward_part.astype(jnp.bfloat16).reshape(shape_back),
            backward_part.astype(jnp.bfloat16).reshape(shape_back),
        ],
        1,
    )
    summed = lax.psum(partials, "tp").astype(jnp.float32)
    own_sums = lax.dynamic_index_in_dim(summed, lax.axis_index("tp"), 0, keepdims=False)
    returned = lax.all_to_all(
        own_sums.astype(jnp.bfloat16), "exp", split_axis=1, concat_axis=1, tiled=True
    ).astype(own_sums.dtype)
    expert_out = returned[0].reshape(experts * slot_count, model_width)
    expert_back = returned[1].reshape(experts * slot_count, model_width)
    picked_out = jnp.take(expert_out, target, axis=0).reshape(tok_rows, top_count, model_width)
    picked_back = jnp.take(expert_back, target, axis=0).reshape(tok_rows, top_count, model_width)
    moe_out = jnp.sum(picked_out * gate_values[:, :, None], 1)
    moe_back = jnp.sum(picked_back * gate_values[:, :, None], 1)
    result = (mixed.astype(jnp.float32) + moe_out).astype(jnp.bfloat16)
    grad_mixed = cotangent.astype(jnp.float32) + moe_back
    next_rows = shifted(grad_mixed[: kernel - 1].astype(jnp.bfloat16), ("exp", "tp"), -1).astype(
        jnp.float32
    )
    extended_grad = jnp.concatenate([grad_mixed, next_rows], 0)
    grad_sum = grad_mixed
    for shift_step in range(kernel):
        grad_sum = (
            grad_sum + conv_weight[shift_step] * extended_grad[shift_step : shift_step + tok_rows]
        )
    return (result, grad_sum.astype(jnp.bfloat16))


def solution(mesh):
    in_specs = (
        P(("exp", "tp"), None),
        P(),
        P(("exp", "tp"), None),
        P(("exp", "tp"), None),
        P(("exp", "tp"), None),
        P("exp", None, "tp"),
        P("exp", None, "tp"),
        P("exp", "tp", None),
    )
    out_specs = (P(("exp", "tp"), None), P(("exp", "tp"), None))
    return jax.shard_map(
        per_device, mesh=mesh, in_specs=in_specs, out_specs=out_specs, check_vma=False
    )
```

profile of v0, /device:TPU:121, one launch (start us, length us, event | category | flops | bytes accessed | tf_op | source)
XLA Modules:
  0.0 404.0 jit_solution(1930475148583040575)
XLA Ops:
  7.2 0.9 slice.55
  8.0 2.0 collective-permute-start
  10.0 0.8 copy.36
  10.8 0.1 eq.30
  10.8 0.1 fusion.52
  11.0 0.2 select_reduce_fusion
  11.1 0.1 reduce_sum.30
  11.2 0.1 copy.38
  11.3 0.1 fusion.53
  11.4 1.1 convolution_convert_fusion
  12.5 0.1 reshape.43
  12.6 0.9 copy.40
  13.6 4.0 all-to-all-start.1
  17.5 1.1 fusion.59
  18.6 0.9 convert_element_type.68
  19.4 0.0 collective-permute-done
  19.5 0.1 fusion.37
  19.6 0.2 convolution_convert_fusion.1
  19.8 0.1 reshape.42
  20.0 0.2 copy.39
  20.2 2.5 all-to-all-done.1
  22.7 7.5 %all_to_all.15 = bf16[4,2,3,4096]{3,1,2,0:T(2,128)(2,1)S(1)} all-to-all(bf16[4,2,3,4096]{3,1,2,0:T(2,128)(2,1)S(1)} %copy.39), channel_id=1, replica_groups=mesh['exp'=4,'tp'=32] {'exp'}, dimensions={0} | all-to-all | bytes 393216 | tf_op jit(solution)/shard_map/all_to_all | solution.py:81
  30.2 0.6 pad_maximum_fusion.1
  30.8 1.1 copy.41
  31.9 0.0 all-gather.3.cloned.1.call-update
  31.9 0.2 all-reduce.2.cloned.1.call-start
  32.1 64.0 %all-gather.3.cloned.1.call-done = bf16[64,4,2,3,4096]{4,1,3,2,0:T(4,128)(2,1)} async-done(((bf16[2,4,2,3,4096]{4,1,3,2,0:T(4,128)(2,1)}), bf16[64,4,2,3,4096]{4,1,3,2,0:T(4,128)(2,1)}) %all-gather.3.cloned.1.call-update) | async-done | bytes 12582928 | tf_op jit(solution)/shard_map/all_gather | solution.py:85
  96.1 11.2 %fusion.57 = (bf16[32,1,4,2,3,4096]{5,2,4,3,1,0:T(4,128)(2,1)}, bf16[32,1,4,2,3,4096]{5,2,4,3,1,0:T(4,128)(2,1)S(1)}) fusion(bf16[32,2,4,2,3,4096]{5,2,4,3,1,0:T(4,128)(2,1)} %bitcast.69), kind=kLoop, calls=%fused_computation.81 | loop fusion | bytes 25165824 | tf_op jit(solution)/shard_map/slice | solution.py:88
  107.3 5.7 %copy.54 = bf16[32,1,4,2,3,4096]{5,2,0,4,3,1:T(4,128)(2,1)} copy(bf16[32,1,4,2,3,4096]{5,2,4,3,1,0:T(4,128)(2,1)S(1)} %get-tuple-element.8) | data formatting | bytes 12582912
  113.0 9.7 %reshape_squeeze.12 = bf16[128,2,3,4096]{3,0,2,1:T(8,128)(2,1)} reshape(bf16[32,1,4,2,3,4096]{5,2,0,4,3,1:T(4,128)(2,1)} %copy.54) | data formatting | bytes 12582912 | tf_op jit(solution)/shard_map/reshape;squeeze | solution.py:87
  122.7 9.4 %fusion.23 = f32[128,2,3,448]{0,3,2,1:T(8,128)} fusion(bf16[128,2,3,4096]{3,0,2,1:T(8,128)(2,1)} %reshape_squeeze.12, bf16[2,4096,448]{1,2,0:T(8,128)(2,1)} %param.15), kind=kOutput, calls=%fused_computation.21 | convolution fusion | flops 2818572288 | bytes 15007744 | tf_op jit(solution)/shard_map/mjsd,jdf->mjsf/dot_general | solution.py:14
  132.1 7.2 %fusion.26 = f32[128,2,3,448]{0,3,2,1:T(8,128)} fusion(bf16[128,2,3,4096]{3,0,2,1:T(8,128)(2,1)S(1)} %copy-done.1, bf16[2,4096,448]{1,2,0:T(8,128)(2,1)} %param.16), kind=kOutput, calls=%fused_computation.22 | convolution fusion | flops 2818572288 | bytes 15007744 | tf_op jit(solution)/shard_map/mjsd,jdf->mjsf/dot_general | solution.py:17
  139.4 5.7 %copy.55 = bf16[32,1,4,2,3,4096]{5,2,0,4,3,1:T(4,128)(2,1)} copy(bf16[32,1,4,2,3,4096]{5,2,4,3,1,0:T(4,128)(2,1)S(1)} %bitcast.66) | data formatting | bytes 12582912
  145.1 9.9 %reshape_squeeze.13 = bf16[128,2,3,4096]{3,0,2,1:T(8,128)(2,1)} reshape(bf16[32,1,4,2,3,4096]{5,2,0,4,3,1:T(4,128)(2,1)} %copy.55) | data formatting | bytes 12582912 | tf_op jit(solution)/shard_map/reshape;squeeze | solution.py:88
  155.0 8.7 %fusion.20 = f32[128,2,3,448]{0,3,2,1:T(8,128)S(1)} fusion(bf16[128,2,3,4096]{3,0,2,1:T(8,128)(2,1)} %reshape_squeeze.13, bf16[2,448,4096]{2,1,0:T(8,128)(2,1)} %param.17), kind=kOutput, calls=%fused_computation.20 | convolution fusion | flops 2818572288 | bytes 15007744 | tf_op jit(solution)/shard_map/mjsd,jfd->mjsf/dot_general | solution.py:24
  163.6 9.8 %fusion.17 = bf16[128,2,3,4096]{3,0,2,1:T(8,128)(2,1)} fusion(bf16[2,448,4096]{2,1,0:T(8,128)(2,1)} %param.17, f32[128,2,3,448]{0,3,2,1:T(8,128)S(1)} %copy-done.4, f32[128,2,3,448]{0,3,2,1:T(8,128)S(1)} %copy-done.2), kind=kOutput, calls=%fused_computation.17 | convolution fusion | flops 2823782400 | bytes 16384000 | tf_op jit(solution)/shard_map/mjsf,jfd->mjsd/dot_general | solution.py:21
  173.4 6.6 %fusion.3 = f32[2,128,3,4096]{3,1,2,0:T(8,128)} fusion(bf16[2,4096,448]{1,2,0:T(8,128)(2,1)S(1)} %bitcast.71, f32[128,2,3,448]{0,3,2,1:T(8,128)S(1)} %copy-done.2, f32[128,2,3,448]{0,3,2,1:T(8,128)S(1)} %fusion.20, f32[128,2,3,448]{0,3,2,1:T(8,128)S(1)} %copy-done.4), kind=kOutput, calls=%fused_computation.7 | convolution fusion | flops 2822012928 | bytes 24051712 | tf_op jit(solution)/shard_map/mjsf,jdf->mjsd/dot_general | solution.py:31
  180.1 11.1 %fusion.14 = bf16[128,2,3,4096]{3,0,2,1:T(8,128)(2,1)S(1)} fusion(f32[2,128,3,4096]{3,1,2,0:T(8,128)} %fusion.3, bf16[2,4096,448]{1,2,0:T(8,128)(2,1)} %param.16, f32[128,2,3,448]{0,3,2,1:T(8,128)} %copy-done.3, f32[128,2,3,448]{0,3,2,1:T(8,128)} %fusion.23), kind=kOutput, calls=%fused_computation.16 | convolution fusion | flops 2826928128 | bytes 28966912 | tf_op jit(solution)/shard_map/mjsf,jdf->mjsd/dot_general | solution.py:33
  191.2 12.8 %copy.53 = bf16[128,2,3,4096]{3,1,2,0:T(2,128)(2,1)S(1)} copy(bf16[128,2,3,4096]{3,0,2,1:T(8,128)(2,1)S(1)} %fusion.14) | data formatting | bytes 12582912 | tf_op jit(solution)/shard_map/stack;reshape | solution.py:93
  204.1 12.8 %copy.52 = bf16[128,2,3,4096]{3,1,2,0:T(2,128)(2,1)S(1)} copy(bf16[128,2,3,4096]{3,0,2,1:T(8,128)(2,1)S(1)} %copy-done) | data formatting | bytes 12582912 | tf_op jit(solution)/shard_map/stack;reshape | solution.py:93
  216.9 18.0 %pad_maximum_fusion = bf16[32,2,4,2,3,4096]{5,3,4,1,2,0:T(2,128)(2,1)} fusion(bf16[32,1,4,2,3,4096]{5,3,4,1,2,0:T(2,128)(2,1)S(1)} %bitcast.67, bf16[32,1,4,2,3,4096]{5,3,4,1,2,0:T(2,128)(2,1)S(1)} %bitcast.68), kind=kLoop, calls=%fused_computation.2 | loop fusion | flops 6291456 | bytes 25165824 | tf_op jit(solution)/shard_map/stack | solution.py:93
  234.9 0.0 all-reduce.2.cloned.1.call-update
  235.0 0.6 copy-done.6
  235.6 0.1 copy.47
  235.7 133.0 %all-reduce.2.cloned.1.call-done = bf16[32,2,4,2,3,4096]{5,3,4,1,2,0:T(2,128)(2,1)} async-done(((bf16[32,2,4,2,3,4096]{5,3,4,1,2,0:T(2,128)(2,1)}), bf16[32,2,4,2,3,4096]{5,3,4,1,2,0:T(2,128)(2,1)}) %all-reduce.2.cloned.1.call-update) | async-done | bytes 12582928 | tf_op jit(solution)/shard_map/psum | solution.py:100
  368.7 2.2 fusion.31
  370.8 4.0 all-to-all-start.2
  374.8 0.0 copy-start.5
  374.8 8.4 %all-to-all-done.2 = bf16[2,4,2,3,4096]{4,2,3,0,1:T(2,128)(2,1)S(1)} async-done(((bf16[2,4,2,3,4096]{4,2,3,0,1:T(2,128)(2,1)}), bf16[2,4,2,3,4096]{4,2,3,0,1:T(2,128)(2,1)S(1)}, u32[]{:S(2)}, u32[]{:S(2)}) %all-to-all-start.2) | async-done | bytes 393248 | tf_op jit(solution)/shard_map/all_to_all | solution.py:102
  383.2 0.3 fusion.58
  383.5 0.3 copy.48
  383.8 0.2 reshape_squeeze.15
  384.0 0.3 copy.46
  384.3 0.2 reshape_squeeze.14
  384.5 0.6 gather_fusion.1
  385.1 0.6 gather_fusion
  385.8 0.1 broadcast_select_fusion.1
  385.9 0.2 reshape.44
  386.1 0.2 reshape.45
  386.2 0.7 multiply_reduce_fusion
  387.0 2.5 collective-permute-start.1
  389.5 0.6 add_convert_fusion.1
  390.2 6.2 %collective-permute-done.1 = bf16[3,4096]{1,0:T(4,128)(2,1)S(1)} collective-permute-done((bf16[3,4096]{1,0:T(4,128)(2,1)S(1)}, bf16[3,4096]{1,0:T(4,128)(2,1)S(1)}, u32[]{:S(2)}, u32[]{:S(2)}) %collective-permute-start.1) | collective-permute-done | bytes 24608 | tf_op jit(solution)/shard_map/ppermute | solution.py:10
  396.4 0.7 fusion.41
  (31 shorter events, 0.1 us)
Async XLA Ops:
  8.0 11.4 %collective-permute-start = (bf16[3,4096]{1,0:T(4,128)(2,1)S(1)}, bf16[3,4096]{1,0:T(4,128)(2,1)S(1)}, u32[]{:S(2)}, u32[]{:S(2)}) collective-permute-start(bf16[3,4096]{1,0:T(4,128)(2,1)S(1)} %slice.55), channel_id=1, source_target_pairs={{0,1},{1,2},{2,3},{3,4},{4,5},{5,6},{6,7},{7,8},{8,9},{9,10},{10,1... | collective-permute-start | bytes 73736 | tf_op jit(solution)/shard_map/ppermute | solution.py:10
  13.6 9.1 %all-to-all-start.1 = ((bf16[4,2,3,4096]{3,1,2,0:T(2,128)(2,1)}), bf16[4,2,3,4096]{3,1,2,0:T(2,128)(2,1)S(1)}, u32[]{:S(2)}, u32[]{:S(2)}) async-start(bf16[4,2,3,4096]{3,1,2,0:T(2,128)(2,1)} %copy.40), calls=%async_computation.1 | async-start | bytes 393216 | tf_op jit(solution)/shard_map/all_to_all | solution.py:82
  17.5 78.6 %all-gather.3.cloned.1.call-start = ((), (), s32[]{:S(2)}) async-start(), calls=%async_computation.4 | async-start | bytes 12976128 | tf_op jit(solution)/shard_map/all_gather | solution.py:85
  31.9 336.8 %all-reduce.2.cloned.1.call-start = ((), (), s32[]{:S(2)}) async-start(), calls=%async_computation.3 | async-start | bytes 25165824 | tf_op jit(solution)/shard_map/psum | solution.py:100
  122.7 9.4 %copy-start.1 = (bf16[128,2,3,4096]{3,0,2,1:T(8,128)(2,1)S(1)}, bf16[128,2,3,4096]{3,0,2,1:T(8,128)(2,1)}, u32[]{:S(2)}) copy-start(bf16[128,2,3,4096]{3,0,2,1:T(8,128)(2,1)} %reshape_squeeze.12) | copy-start | bytes 18874372
  122.7 16.7 %slice-start = ((s8[6291456]{0:T(1024)(128)(4,1)}), s8[4194304]{0:T(1024)(128)(4,1)S(1)}, s32[]{:S(2)}) async-start(s8[6291456]{0:T(1024)(128)(4,1)} %bitcast.65), calls=%async_computation.5 | async-start | bytes 8388608
  132.1 7.2 %slice-start.1 = ((s8[6291456]{0:T(1024)(128)(4,1)}), s8[2097152]{0:T(1024)(128)(4,1)S(1)}, s32[]{:S(2)}) async-start(s8[6291456]{0:T(1024)(128)(4,1)} %bitcast.65), calls=%async_computation.6 | async-start | bytes 4194304
  145.1 28.3 %slice-start.2 = ((s8[7340032]{0:T(1024)(128)(4,1)}), s8[3145728]{0:T(1024)(128)(4,1)S(1)}, s32[]{:S(2)}) async-start(s8[7340032]{0:T(1024)(128)(4,1)} %bitcast.70), calls=%async_computation.7 | async-start | bytes 6291456
  155.0 8.7 %copy-start.2 = (f32[128,2,3,448]{0,3,2,1:T(8,128)S(1)}, f32[128,2,3,448]{0,3,2,1:T(8,128)}, u32[]{:S(2)}) copy-start(f32[128,2,3,448]{0,3,2,1:T(8,128)} %fusion.23) | copy-start | bytes 4128772
  155.0 8.7 %copy-start.4 = (f32[128,2,3,448]{0,3,2,1:T(8,128)S(1)}, f32[128,2,3,448]{0,3,2,1:T(8,128)}, u32[]{:S(2)}) copy-start(f32[128,2,3,448]{0,3,2,1:T(8,128)} %fusion.26) | copy-start | bytes 4128772
  155.0 18.5 %slice-start.3 = ((s8[7340032]{0:T(1024)(128)(4,1)}), s8[4194304]{0:T(1024)(128)(4,1)S(1)}, s32[]{:S(2)}) async-start(s8[7340032]{0:T(1024)(128)(4,1)} %bitcast.70), calls=%async_computation.8 | async-start | bytes 8388608
  163.6 9.8 %copy-start.3 = (f32[128,2,3,448]{0,3,2,1:T(8,128)}, f32[128,2,3,448]{0,3,2,1:T(8,128)S(1)}, u32[]{:S(2)}) copy-start(f32[128,2,3,448]{0,3,2,1:T(8,128)S(1)} %fusion.20) | copy-start | bytes 4128772
  191.2 12.9 %copy-start = (bf16[128,2,3,4096]{3,0,2,1:T(8,128)(2,1)S(1)}, bf16[128,2,3,4096]{3,0,2,1:T(8,128)(2,1)}, u32[]{:S(2)}) copy-start(bf16[128,2,3,4096]{3,0,2,1:T(8,128)(2,1)} %fusion.17) | copy-start | bytes 18874372
  234.9 0.7 copy-start.6
  370.8 12.4 %all-to-all-start.2 = ((bf16[2,4,2,3,4096]{4,2,3,0,1:T(2,128)(2,1)}), bf16[2,4,2,3,4096]{4,2,3,0,1:T(2,128)(2,1)S(1)}, u32[]{:S(2)}, u32[]{:S(2)}) async-start(bf16[2,4,2,3,4096]{4,2,3,0,1:T(2,128)(2,1)} %fusion.31), calls=%async_computation.2 | async-start | bytes 786432 | tf_op jit(solution)/shard_map/all_to_all | solution.py:102
  374.8 12.1 %copy-start.5 = (bf16[8,4096]{1,0:T(8,128)(2,1)S(1)}, bf16[8,4096]{1,0:T(8,128)(2,1)}, u32[]{:S(2)}) copy-start(bf16[8,4096]{1,0:T(8,128)(2,1)} %param.14) | copy-start | bytes 196612
  387.0 9.5 %collective-permute-start.1 = (bf16[3,4096]{1,0:T(4,128)(2,1)S(1)}, bf16[3,4096]{1,0:T(4,128)(2,1)S(1)}, u32[]{:S(2)}, u32[]{:S(2)}) collective-permute-start(bf16[3,4096]{1,0:T(4,128)(2,1)S(1)} %slice.127), channel_id=1, source_target_pairs={{1,0},{2,1},{3,2},{4,3},{5,4},{6,5},{7,6},{8,7},{9,8},{10,9},{11,1... | collective-permute-start | bytes 73736 | tf_op jit(solution)/shard_map/ppermute | solution.py:10
Sparse Core Ops, SparseCore 0:
  32.0 64.0 all-gather.2
  235.1 133.5 all-reduce.1
where the time goes:
time: 405 us; the launch traced here: 404 us
  waiting for transfers between devices  214 us (53%)
  local copies, waits for them, and re-layouts  76.9 us (19%)
  matrix products  54.2 us (13%)
  other arithmetic  24.4 us (6%)
  between operations  14.3 us (4%)
  starting transfers between devices  12.7 us (3%)
  blocking collectives  7.53 us (2%)
    psum x1, waiting for transfers between devices, per_device(): summed = lax.psum(partials, 'tp').astype(jnp.float32)  133 us
    all_gather x1, waiting for transfers between devices, per_device(): piece = lax.all_gather(stacked, 'tp', axis=0, tiled=True)  64 us
    another operation x2, local copies, waits for them, and re-layouts, per_device(): jnp.stack([forward_part.astype(jnp.bfloat16).reshape(shape_back), backwar...  25.7 us
    another operation x1, other arithmetic, per_device(): jnp.stack([forward_part.astype(jnp.bfloat16).reshape(shape_back), backwar...  18 us
    unnamed x26, local copies, waits for them, and re-layouts  13 us
    slice x1, local copies, waits for them, and re-layouts, per_device(): piece[:, 1].reshape(piece_rows * groups, per_group, slot_count, model_width)  11.2 us
    dot_general x1, matrix products, expert_rows(): jnp.einsum('mjsf,jdf->mjsd', grad_up, up_weight, preferred_element_type=j...  11.1 us
    another operation x1, local copies, waits for them, and re-layouts, per_device(): piece[:, 1].reshape(piece_rows * groups, per_group, slot_count, model_width)  9.86 us
  transfers between devices with their start and end apart: 6, of which 5 were waited for; matrix products, arithmetic and copies ran while one was open for 2% of the time, Pallas kernels for 0%

commit v1 on v0

--- a/solution.py
+++ b/solution.py
@@ -82,7 +82,9 @@
         lax.all_to_all(packed_grad, "exp", split_axis=0, concat_axis=0, tiled=True),
     )
     stacked = jnp.stack([recv_in, recv_grad], 0)[None]
-    piece = lax.all_gather(stacked, "tp", axis=0, tiled=True)
+    piece = jnp.concatenate(
+        lax.all_to_all(jnp.stack([stacked for _ in range(lax.axis_size("tp"))]), "tp", 0, 0), axis=0
+    )
     piece_rows = piece.shape[0]
     rows_in = piece[:, 0].reshape(piece_rows * groups, per_group, slot_count, model_width)
     rows_grad = piece[:, 1].reshape(piece_rows * groups, per_group, slot_count, model_width)

time: 405 us -> 490 us (1.21)
  blocking collectives: 7.53 us -> 158 us
  waiting for transfers between devices: 214 us -> 148 us
    all_to_all x0 -> x1, blocking collectives: none -> 151 us  [per_device(): lax.all_to_all(jnp.stack([stacked for _ in range(lax.axis_size('tp'))]),...]
    all_gather x1 -> x0, waiting for transfers between devices: 64 us -> none  [per_device(): piece = lax.all_gather(stacked, 'tp', axis=0, tiled=True)]
    unnamed x26 -> x24, local copies, waits for them, and re-layouts: 13 us -> 1.53 us
    another operation x0 -> x1, local copies, waits for them, and re-layouts: none -> 5.88 us  [per_device(): jnp.stack([stacked for _ in range(lax.axis_size('tp'))])]
    slice x0 -> x1, local copies, waits for them, and re-layouts: none -> 5.66 us  [per_device(): piece[:, 0].reshape(piece_rows * groups, per_group, slot_count, model_width)]
    slice x1 -> x2, local copies, waits for them, and re-layouts: 11.2 us -> 12.1 us  [per_device(): piece[:, 1].reshape(piece_rows * groups, per_group, slot_count, model_width)]
  transfers between devices with their start and end apart: 6 -> 5, of which waited for: 5 -> 4; matrix products, arithmetic and copies ran while one was open for 2% -> 1% of each run, Pallas kernels for 0% -> 0%
where the time goes in v1:
time: 490 us; the launch traced here: 489 us
  blocking collectives  158 us (32%)
  waiting for transfers between devices  148 us (30%)
  local copies, waits for them, and re-layouts  77.1 us (16%)
  matrix products  54.4 us (11%)
  other arithmetic  24.3 us (5%)
  between operations  14.3 us (3%)
  starting transfers between devices  12.5 us (3%)
    all_to_all x1, blocking collectives, per_device(): lax.all_to_all(jnp.stack([stacked for _ in range(lax.axis_size('tp'))]),...  151 us
    psum x1, waiting for transfers between devices, per_device(): summed = lax.psum(partials, 'tp').astype(jnp.float32)  131 us
    another operation x2, local copies, waits for them, and re-layouts, per_device(): jnp.stack([forward_part.astype(jnp.bfloat16).reshape(shape_back), backwar...  25.7 us
    another operation x1, other arithmetic, per_device(): jnp.stack([forward_part.astype(jnp.bfloat16).reshape(shape_back), backwar...  18 us
    slice x2, local copies, waits for them, and re-layouts, per_device(): piece[:, 1].reshape(piece_rows * groups, per_group, slot_count, model_width)  12.1 us
    dot_general x1, matrix products, expert_rows(): jnp.einsum('mjsf,jdf->mjsd', grad_up, up_weight, preferred_element_type=j...  11.1 us
    another operation x1, local copies, waits for them, and re-layouts, per_device(): piece[:, 1].reshape(piece_rows * groups, per_group, slot_count, model_width)  9.85 us
  transfers between devices with their start and end apart: 5, of which 4 were waited for; matrix products, arithmetic and copies ran while one was open for 1% of the time, Pallas kernels for 0%

profile of v1, /device:TPU:121, one launch (start us, length us, event | category | flops | bytes accessed | tf_op | source)
XLA Modules:
  0.0 488.8 jit_solution(470950605922124631)
XLA Ops:
  7.2 0.9 slice.55
  8.0 2.0 collective-permute-start
  10.0 0.8 copy.34
  10.8 0.1 eq.30
  10.8 0.1 fusion.52
  11.0 0.2 select_reduce_fusion
  11.1 0.1 reduce_sum.30
  11.2 0.1 copy.36
  11.3 0.1 fusion.53
  11.4 1.1 convolution_convert_fusion
  12.5 0.1 reshape.48
  12.6 0.9 copy.38
  13.6 4.0 all-to-all-start.1
  17.5 1.1 fusion.59
  18.6 0.9 convert_element_type.68
  19.4 0.0 collective-permute-done
  19.5 0.1 fusion.37
  19.6 0.2 convolution_convert_fusion.1
  19.8 0.1 reshape.47
  20.0 0.2 copy.37
  20.2 2.5 all-to-all-done.1
  22.7 7.5 %all_to_all.20 = bf16[4,2,3,4096]{3,1,2,0:T(2,128)(2,1)S(1)} all-to-all(bf16[4,2,3,4096]{3,1,2,0:T(2,128)(2,1)S(1)} %copy.37), channel_id=1, replica_groups=mesh['exp'=4,'tp'=32] {'exp'}, dimensions={0} | all-to-all | bytes 393216 | tf_op jit(solution)/shard_map/all_to_all | solution.py:81
  30.2 0.6 pad_maximum_fusion.1
  30.8 0.3 copy.39
  31.1 5.9 %stack.18 = bf16[32,1,2,4,2,3,4096]{6,3,5,4,2,1,0:T(4,128)(2,1)S(1)} broadcast(bf16[2,4,2,3,4096]{4,1,3,2,0:T(4,128)(2,1)S(1)} %copy.39), dimensions={2,3,4,5,6} | broadcast | bytes 12976128 | tf_op jit(solution)/shard_map/stack | solution.py:86
  37.0 150.6 %all_to_all.21 = bf16[32,1,2,4,2,3,4096]{6,3,5,4,2,1,0:T(4,128)(2,1)S(1)} all-to-all(bf16[32,1,2,4,2,3,4096]{6,3,5,4,2,1,0:T(4,128)(2,1)S(1)} %stack.18), channel_id=1, replica_groups=mesh['exp'=4,'tp'=32] {'tp'}, dimensions={0} | all-to-all | bytes 25165824 | tf_op jit(solution)/shard_map/all_to_all | solution.py:86
  187.6 6.4 %fusion.57 = (bf16[32,1,4,2,3,4096]{5,2,4,3,1,0:T(4,128)(2,1)}, bf16[32,1,4,2,3,4096]{5,2,4,3,1,0:T(4,128)(2,1)S(1)}) fusion(bf16[32,2,4,2,3,4096]{5,2,4,3,1,0:T(4,128)(2,1)S(1)} %bitcast.65), kind=kLoop, calls=%fused_computation.81 | loop fusion | bytes 25165824 | tf_op jit(solution)/shard_map/slice | solution.py:90
  194.0 5.7 %copy.40 = bf16[32,1,4,2,3,4096]{5,2,0,4,3,1:T(4,128)(2,1)} copy(bf16[32,1,4,2,3,4096]{5,2,4,3,1,0:T(4,128)(2,1)S(1)} %get-tuple-element.8) | data formatting | bytes 12582912 | tf_op jit(solution)/shard_map/slice | solution.py:89
  199.6 9.7 %reshape_squeeze.12 = bf16[128,2,3,4096]{3,0,2,1:T(8,128)(2,1)} reshape(bf16[32,1,4,2,3,4096]{5,2,0,4,3,1:T(4,128)(2,1)} %copy.40) | data formatting | bytes 12582912 | tf_op jit(solution)/shard_map/reshape;squeeze | solution.py:89
  209.4 9.7 %fusion.23 = f32[128,2,3,448]{0,3,2,1:T(8,128)} fusion(bf16[128,2,3,4096]{3,0,2,1:T(8,128)(2,1)} %reshape_squeeze.12, bf16[2,4096,448]{1,2,0:T(8,128)(2,1)} %param.15), kind=kOutput, calls=%fused_computation.21 | convolution fusion | flops 2818572288 | bytes 15007744 | tf_op jit(solution)/shard_map/mjsd,jdf->mjsf/dot_general | solution.py:14
  219.1 0.0 copy-done.1
  219.1 7.2 %fusion.26 = f32[128,2,3,448]{0,3,2,1:T(8,128)} fusion(bf16[128,2,3,4096]{3,0,2,1:T(8,128)(2,1)S(1)} %copy-done.1, bf16[2,4096,448]{1,2,0:T(8,128)(2,1)} %param.16), kind=kOutput, calls=%fused_computation.22 | convolution fusion | flops 2818572288 | bytes 15007744 | tf_op jit(solution)/shard_map/mjsd,jdf->mjsf/dot_general | solution.py:17
  226.3 5.7 %copy.41 = bf16[32,1,4,2,3,4096]{5,2,0,4,3,1:T(4,128)(2,1)} copy(bf16[32,1,4,2,3,4096]{5,2,4,3,1,0:T(4,128)(2,1)S(1)} %bitcast.67) | data formatting | bytes 12582912 | tf_op jit(solution)/shard_map/slice | solution.py:90
  232.0 9.8 %reshape_squeeze.13 = bf16[128,2,3,4096]{3,0,2,1:T(8,128)(2,1)} reshape(bf16[32,1,4,2,3,4096]{5,2,0,4,3,1:T(4,128)(2,1)} %copy.41) | data formatting | bytes 12582912 | tf_op jit(solution)/shard_map/reshape;squeeze | solution.py:90
  241.9 8.7 %fusion.20 = f32[128,2,3,448]{0,3,2,1:T(8,128)S(1)} fusion(bf16[128,2,3,4096]{3,0,2,1:T(8,128)(2,1)} %reshape_squeeze.13, bf16[2,448,4096]{2,1,0:T(8,128)(2,1)} %param.17), kind=kOutput, calls=%fused_computation.20 | convolution fusion | flops 2818572288 | bytes 15007744 | tf_op jit(solution)/shard_map/mjsd,jfd->mjsf/dot_general | solution.py:24
  250.6 9.8 %fusion.17 = bf16[128,2,3,4096]{3,0,2,1:T(8,128)(2,1)} fusion(bf16[2,448,4096]{2,1,0:T(8,128)(2,1)} %param.17, f32[128,2,3,448]{0,3,2,1:T(8,128)S(1)} %copy-done.4, f32[128,2,3,448]{0,3,2,1:T(8,128)S(1)} %copy-done.2), kind=kOutput, calls=%fused_computation.17 | convolution fusion | flops 2823782400 | bytes 16384000 | tf_op jit(solution)/shard_map/mjsf,jfd->mjsd/dot_general | solution.py:21
  260.3 6.6 %fusion.3 = f32[2,128,3,4096]{3,1,2,0:T(8,128)} fusion(bf16[2,4096,448]{1,2,0:T(8,128)(2,1)S(1)} %bitcast.71, f32[128,2,3,448]{0,3,2,1:T(8,128)S(1)} %copy-done.2, f32[128,2,3,448]{0,3,2,1:T(8,128)S(1)} %fusion.20, f32[128,2,3,448]{0,3,2,1:T(8,128)S(1)} %copy-done.4), kind=kOutput, calls=%fused_computation.7 | convolution fusion | flops 2822012928 | bytes 24051712 | tf_op jit(solution)/shard_map/mjsf,jdf->mjsd/dot_general | solution.py:31
  267.0 11.1 %fusion.14 = bf16[128,2,3,4096]{3,0,2,1:T(8,128)(2,1)S(1)} fusion(f32[2,128,3,4096]{3,1,2,0:T(8,128)} %fusion.3, bf16[2,4096,448]{1,2,0:T(8,128)(2,1)} %param.16, f32[128,2,3,448]{0,3,2,1:T(8,128)} %copy-done.3, f32[128,2,3,448]{0,3,2,1:T(8,128)} %fusion.23), kind=kOutput, calls=%fused_computation.16 | convolution fusion | flops 2826928128 | bytes 28966912 | tf_op jit(solution)/shard_map/mjsf,jdf->mjsd/dot_general | solution.py:33
  278.1 12.8 %copy.51 = bf16[128,2,3,4096]{3,1,2,0:T(2,128)(2,1)S(1)} copy(bf16[128,2,3,4096]{3,0,2,1:T(8,128)(2,1)S(1)} %fusion.14) | data formatting | bytes 12582912 | tf_op jit(solution)/shard_map/stack;reshape | solution.py:95
  291.0 12.8 %copy.50 = bf16[128,2,3,4096]{3,1,2,0:T(2,128)(2,1)S(1)} copy(bf16[128,2,3,4096]{3,0,2,1:T(8,128)(2,1)S(1)} %copy-done) | data formatting | bytes 12582912 | tf_op jit(solution)/shard_map/stack;reshape | solution.py:95
  303.8 18.0 %pad_maximum_fusion = bf16[32,2,4,2,3,4096]{5,3,4,1,2,0:T(2,128)(2,1)} fusion(bf16[32,1,4,2,3,4096]{5,3,4,1,2,0:T(2,128)(2,1)S(1)} %bitcast.68, bf16[32,1,4,2,3,4096]{5,3,4,1,2,0:T(2,128)(2,1)S(1)} %bitcast.69), kind=kLoop, calls=%fused_computation.2 | loop fusion | flops 6291456 | bytes 25165824 | tf_op jit(solution)/shard_map/stack | solution.py:95
  321.9 0.0 all-reduce.2.cloned.1.call-update
  321.9 0.6 copy-done.6
  322.5 0.1 copy.45
  322.6 130.8 %all-reduce.2.cloned.1.call-done = bf16[32,2,4,2,3,4096]{5,3,4,1,2,0:T(2,128)(2,1)} async-done(((bf16[32,2,4,2,3,4096]{5,3,4,1,2,0:T(2,128)(2,1)}), bf16[32,2,4,2,3,4096]{5,3,4,1,2,0:T(2,128)(2,1)}) %all-reduce.2.cloned.1.call-update) | async-done | bytes 12582928 | tf_op jit(solution)/shard_map/psum | solution.py:102
  453.4 2.1 fusion.31
  455.6 4.0 all-to-all-start.3
  459.6 0.0 copy-start.5
  459.6 8.4 %all-to-all-done.3 = bf16[2,4,2,3,4096]{4,2,3,0,1:T(2,128)(2,1)S(1)} async-done(((bf16[2,4,2,3,4096]{4,2,3,0,1:T(2,128)(2,1)}), bf16[2,4,2,3,4096]{4,2,3,0,1:T(2,128)(2,1)S(1)}, u32[]{:S(2)}, u32[]{:S(2)}) %all-to-all-start.3) | async-done | bytes 393248 | tf_op jit(solution)/shard_map/all_to_all | solution.py:104
  467.9 0.3 fusion.58
  468.3 0.3 copy.46
  468.5 0.2 reshape_squeeze.15
  468.8 0.3 copy.44
  469.0 0.2 reshape_squeeze.14
  469.2 0.6 gather_fusion.1
  469.9 0.6 gather_fusion
  470.5 0.1 broadcast_select_fusion.1
  470.6 0.2 reshape.50
  470.8 0.2 reshape.51
  471.0 0.7 multiply_reduce_fusion
  471.7 2.5 collective-permute-start.1
  474.3 0.6 add_convert_fusion.1
  474.9 6.2 %collective-permute-done.1 = bf16[3,4096]{1,0:T(4,128)(2,1)S(1)} collective-permute-done((bf16[3,4096]{1,0:T(4,128)(2,1)S(1)}, bf16[3,4096]{1,0:T(4,128)(2,1)S(1)}, u32[]{:S(2)}, u32[]{:S(2)}) %collective-permute-start.1) | collective-permute-done | bytes 24608 | tf_op jit(solution)/shard_map/ppermute | solution.py:10
  481.2 0.7 fusion.41
  (30 shorter events, 0.1 us)
Async XLA Ops:
  8.0 11.4 %collective-permute-start = (bf16[3,4096]{1,0:T(4,128)(2,1)S(1)}, bf16[3,4096]{1,0:T(4,128)(2,1)S(1)}, u32[]{:S(2)}, u32[]{:S(2)}) collective-permute-start(bf16[3,4096]{1,0:T(4,128)(2,1)S(1)} %slice.55), channel_id=1, source_target_pairs={{0,1},{1,2},{2,3},{3,4},{4,5},{5,6},{6,7},{7,8},{8,9},{9,10},{10,1... | collective-permute-start | bytes 73736 | tf_op jit(solution)/shard_map/ppermute | solution.py:10
  13.6 9.1 %all-to-all-start.1 = ((bf16[4,2,3,4096]{3,1,2,0:T(2,128)(2,1)}), bf16[4,2,3,4096]{3,1,2,0:T(2,128)(2,1)S(1)}, u32[]{:S(2)}, u32[]{:S(2)}) async-start(bf16[4,2,3,4096]{3,1,2,0:T(2,128)(2,1)} %copy.38), calls=%async_computation.1 | async-start | bytes 393216 | tf_op jit(solution)/shard_map/all_to_all | solution.py:82
  17.5 435.9 %all-reduce.2.cloned.1.call-start = ((), (), s32[]{:S(2)}) async-start(), calls=%async_computation.4 | async-start | bytes 25165824 | tf_op jit(solution)/shard_map/psum | solution.py:102
  209.3 9.7 %copy-start.1 = (bf16[128,2,3,4096]{3,0,2,1:T(8,128)(2,1)S(1)}, bf16[128,2,3,4096]{3,0,2,1:T(8,128)(2,1)}, u32[]{:S(2)}) copy-start(bf16[128,2,3,4096]{3,0,2,1:T(8,128)(2,1)} %reshape_squeeze.12) | copy-start | bytes 18874372
  209.4 16.9 %slice-start = ((s8[6291456]{0:T(1024)(128)(4,1)}), s8[4194304]{0:T(1024)(128)(4,1)S(1)}, s32[]{:S(2)}) async-start(s8[6291456]{0:T(1024)(128)(4,1)} %bitcast.66), calls=%async_computation.5 | async-start | bytes 8388608
  219.1 7.2 %slice-start.1 = ((s8[6291456]{0:T(1024)(128)(4,1)}), s8[2097152]{0:T(1024)(128)(4,1)S(1)}, s32[]{:S(2)}) async-start(s8[6291456]{0:T(1024)(128)(4,1)} %bitcast.66), calls=%async_computation.6 | async-start | bytes 4194304
  232.0 28.3 %slice-start.2 = ((s8[7340032]{0:T(1024)(128)(4,1)}), s8[3145728]{0:T(1024)(128)(4,1)S(1)}, s32[]{:S(2)}) async-start(s8[7340032]{0:T(1024)(128)(4,1)} %bitcast.70), calls=%async_computation.7 | async-start | bytes 6291456
  241.9 8.7 %copy-start.2 = (f32[128,2,3,448]{0,3,2,1:T(8,128)S(1)}, f32[128,2,3,448]{0,3,2,1:T(8,128)}, u32[]{:S(2)}) copy-start(f32[128,2,3,448]{0,3,2,1:T(8,128)} %fusion.23) | copy-start | bytes 4128772
  241.9 8.7 %copy-start.4 = (f32[128,2,3,448]{0,3,2,1:T(8,128)S(1)}, f32[128,2,3,448]{0,3,2,1:T(8,128)}, u32[]{:S(2)}) copy-start(f32[128,2,3,448]{0,3,2,1:T(8,128)} %fusion.26) | copy-start | bytes 4128772
  241.9 18.5 %slice-start.3 = ((s8[7340032]{0:T(1024)(128)(4,1)}), s8[4194304]{0:T(1024)(128)(4,1)S(1)}, s32[]{:S(2)}) async-start(s8[7340032]{0:T(1024)(128)(4,1)} %bitcast.70), calls=%async_computation.8 | async-start | bytes 8388608
  250.6 9.8 %copy-start.3 = (f32[128,2,3,448]{0,3,2,1:T(8,128)}, f32[128,2,3,448]{0,3,2,1:T(8,128)S(1)}, u32[]{:S(2)}) copy-start(f32[128,2,3,448]{0,3,2,1:T(8,128)S(1)} %fusion.20) | copy-start | bytes 4128772
  278.1 12.9 %copy-start = (bf16[128,2,3,4096]{3,0,2,1:T(8,128)(2,1)S(1)}, bf16[128,2,3,4096]{3,0,2,1:T(8,128)(2,1)}, u32[]{:S(2)}) copy-start(bf16[128,2,3,4096]{3,0,2,1:T(8,128)(2,1)} %fusion.17) | copy-start | bytes 18874372
  321.9 0.7 copy-start.6
  455.6 12.4 %all-to-all-start.3 = ((bf16[2,4,2,3,4096]{4,2,3,0,1:T(2,128)(2,1)}), bf16[2,4,2,3,4096]{4,2,3,0,1:T(2,128)(2,1)S(1)}, u32[]{:S(2)}, u32[]{:S(2)}) async-start(bf16[2,4,2,3,4096]{4,2,3,0,1:T(2,128)(2,1)} %fusion.31), calls=%async_computation.3 | async-start | bytes 786432 | tf_op jit(solution)/shard_map/all_to_all | solution.py:104
  459.6 12.1 %copy-start.5 = (bf16[8,4096]{1,0:T(8,128)(2,1)S(1)}, bf16[8,4096]{1,0:T(8,128)(2,1)}, u32[]{:S(2)}) copy-start(bf16[8,4096]{1,0:T(8,128)(2,1)} %param.14) | copy-start | bytes 196612
  471.7 9.5 %collective-permute-start.1 = (bf16[3,4096]{1,0:T(4,128)(2,1)S(1)}, bf16[3,4096]{1,0:T(4,128)(2,1)S(1)}, u32[]{:S(2)}, u32[]{:S(2)}) collective-permute-start(bf16[3,4096]{1,0:T(4,128)(2,1)S(1)} %slice.127), channel_id=1, source_target_pairs={{1,0},{2,1},{3,2},{4,3},{5,4},{6,5},{7,6},{8,7},{9,8},{10,9},{11,1... | collective-permute-start | bytes 73736 | tf_op jit(solution)/shard_map/ppermute | solution.py:10
Sparse Core Ops, SparseCore 0:
  322.0 131.3 all-reduce.1
